TPU v7x, 256 devices: a whole 4x4x8 slice. The times are simulated.
256 devices in a mesh: blk: 64 (over y, z, x_hi), bin: 4 (over x_lo, core).
Axes of the slice: x: 4 (x_hi: 2, x_lo: 2; x = x_hi * 2 + x_lo), y: 4, z: 8, core: 2. Of those that a mesh axis runs over, the one named last changes fastest.
Arguments:
- spectrum: float32 [64, 8, 12, 512, 128], P('bin', None, None, 'blk'), may hold values from 0.05 to 2
- wind: float32 [8, 12, 128], replicated, may hold values from -12 to 12
- fall_speed: float32 [64], P('bin'), may hold values from 0.1 to 10
- collection: bfloat16 [64, 64, 64], P(None, None, 'bin'), may hold values from -0.09375 to 0.09375
- act_order: int32 [64, 8], P('blk'), may hold values from 0 to 7, each once within a row
- act_count: int32 [64], P('blk'), may hold values from 1 to 4, as said below
Outputs:
- updated: float32 [64, 8, 12, 512, 128], P('bin', None, None, 'blk')
Inputs may be any that keep to these rules, and one draw needn't show every extreme that they name: `act_order`: each row names every block row once; the active ones are its first act_count entries. `act_count`: some column holds exactly half of 8 active blocks.
All inputs are finite; a program needn't handle non-finite values.
Results may differ from a plain program's by a relative error of at most 0.0055.
Values may be sent and summed in bfloat16 or wider, within the bound.
A program may use at most 128 MiB of HBM per device.

v0:
```python
import jax
import jax.numpy as jnp
from jax import lax
from jax.sharding import PartitionSpec as P

weno_eps = 1e-06
courant = 0.04
time_step = 2.0


def padded_2(cells, sides, width):
    for axis, dim in sides:
        count = lax.axis_size(axis)
        ends = count - 1
        head = lax.slice_in_dim(cells, 0, width, axis=dim)
        tail = lax.slice_in_dim(cells, cells.shape[dim] - width, cells.shape[dim], axis=dim)
        cells = jnp.concatenate(
            [
                lax.ppermute(tail, axis, [(i, (i + 1) % count) for i in range(ends)]),
                cells,
                lax.ppermute(head, axis, [((i + 1) % count, i) for i in range(ends)]),
            ],
            axis=dim,
        )
    return cells


def reconstruct(first, second, third, fourth, fifth):
    cand_left = (2.0 * first - 7.0 * second + 11.0 * third) / 6.0
    cand_mid = (-second + 5.0 * third + 2.0 * fourth) / 6.0
    cand_right = (2.0 * third + 5.0 * fourth - fifth) / 6.0
    smooth_left = (
        13.0 / 12.0 * (first - 2.0 * second + third) ** 2
        + 0.25 * (first - 4.0 * second + 3.0 * third) ** 2
    )
    smooth_mid = 13.0 / 12.0 * (second - 2.0 * third + fourth) ** 2 + 0.25 * (second - fourth) ** 2
    smooth_right = (
        13.0 / 12.0 * (third - 2.0 * fourth + fifth) ** 2
        + 0.25 * (3.0 * third - 4.0 * fourth + fifth) ** 2
    )
    weight_left = 0.1 / (weno_eps + smooth_left) ** 2
    weight_mid = 0.6 / (weno_eps + smooth_mid) ** 2
    weight_right = 0.3 / (weno_eps + smooth_right) ** 2
    total = weight_left + weight_mid + weight_right
    return (weight_left * cand_left + weight_mid * cand_mid + weight_right * cand_right) / total


def face_terms(padded, width, wind):

    def window(offset):
        return lax.slice_in_dim(padded, offset, offset + width + 1, axis=3)

    upwind_pos = reconstruct(window(0), window(1), window(2), window(3), window(4))
    upwind_neg = reconstruct(window(5), window(4), window(3), window(2), window(1))
    speed = wind[None, :, :, None, :]
    return (speed, speed * upwind_pos, speed * upwind_neg)


def sediment(field, fall_speed):
    above = jnp.concatenate([field[:, :, 1:], jnp.zeros_like(field[:, :, :1])], axis=2)
    return field - courant * fall_speed[:, None, None, None, None] * (field - above)


def collide(spectra, table):
    count_in = spectra.shape[0]
    planes = spectra.shape[1] * spectra.shape[2]
    flat = spectra.reshape(count_in, planes, -1)
    out_bins = table.shape[1] // count_in

    def one_plane(index):
        cells = lax.dynamic_index_in_dim(flat, index, 1, keepdims=False)
        inner = lax.dot_general(
            table, cells, (((0,), (0,)), ((), ())), preferred_element_type=jnp.float32
        )
        inner = inner.astype(jnp.bfloat16).reshape(count_in, out_bins, -1)
        return jnp.einsum("ic,ikc->kc", cells, inner, preferred_element_type=jnp.float32)

    result = lax.map(one_plane, jnp.arange(planes, dtype=jnp.int32))
    return jnp.moveaxis(result, 0, 1).reshape((out_bins,) + spectra.shape[1:])


def local(spectrum, wind, fall_speed, collection, act_order, act_count):
    width = spectrum.shape[3]
    padded = padded_2(spectrum, (("blk", 3),), 3)
    speed, flux_pos, flux_neg = face_terms(padded, width, wind)
    flux = jnp.where(speed > 0, flux_pos, flux_neg)
    advected = spectrum - courant * (flux[:, :, :, 1:, :] - flux[:, :, :, :-1, :])
    settled = sediment(advected, fall_speed)
    slots = spectrum.shape[1]
    capacity = slots // 2
    order = act_order[0, :capacity]
    picked = jnp.take(settled, order, axis=1).astype(jnp.bfloat16)
    all_bins = collection.shape[0]
    whole = lax.all_gather(picked, "bin", axis=0, tiled=True)
    tendency = collide(whole, collection.reshape(all_bins, -1))
    entries = jnp.arange(capacity, dtype=jnp.int32)
    slot_ids = jnp.arange(slots, dtype=jnp.int32)
    chosen = jnp.logical_and(order[:, None] == slot_ids[None, :], (entries < act_count[0])[:, None])
    update = jnp.einsum("as,bazxy->bszxy", chosen.astype(jnp.float32), tendency)
    return settled + time_step * update


def solution(mesh):
    return jax.shard_map(
        local,
        mesh=mesh,
        in_specs=(
            P("bin", None, None, "blk", None),
            P(),
            P("bin"),
            P(None, None, "bin"),
            P("blk", None),
            P("blk"),
        ),
        out_specs=P("bin", None, None, "blk", None),
        check_vma=False,
    )
```

profile of v0, /device:TPU:1, one launch (start us, length us, event | category | flops | bytes accessed | tf_op | source)
XLA Modules:
  0.0 556.1 jit_solution(7151124852510900609)
XLA Ops:
  6.5 6.3 %fusion.39 = (f32[16,8,12,3,128]{4,3,2,1,0:T(4,128)S(1)}, f32[16,8,12,3,128]{4,3,2,1,0:T(4,128)S(1)}) fusion(f32[16,8,12,8,128]{4,3,2,1,0:T(8,128)} %param.8), kind=kLoop, calls=%fused_computation.63 | loop fusion | bytes 9437184 | tf_op jit(solution)/shard_map/slice | solution.py:16
  13.6 5.6 %collective-permute-start = (f32[16,8,12,3,128]{4,1,3,2,0:T(8,128)S(1)}, f32[16,8,12,3,128]{4,1,3,2,0:T(8,128)S(1)}, u32[]{:S(2)}, u32[]{:S(2)}) collective-permute-start(f32[16,8,12,3,128]{4,1,3,2,0:T(8,128)S(1)} %copy.47), channel_id=1, source_target_pairs={{0,4},{4,8},{8,12},{12,16},{16,20},{20,24},{24,28},{28,32},{32,36}... | collective-permute-start | bytes 7077896 | tf_op jit(solution)/shard_map/ppermute | solution.py:19
  19.2 2.2 copy.46
  22.8 96.8 %collective-permute-done = f32[16,8,12,3,128]{4,1,3,2,0:T(8,128)S(1)} collective-permute-done((f32[16,8,12,3,128]{4,1,3,2,0:T(8,128)S(1)}, f32[16,8,12,3,128]{4,1,3,2,0:T(8,128)S(1)}, u32[]{:S(2)}, u32[]{:S(2)}) %collective-permute-start) | collective-permute-done | bytes 2359328 | tf_op jit(solution)/shard_map/ppermute | solution.py:19
  119.7 7.7 %constant_dynamic-update-slice_fusion = (f32[16,8,12,11,128]{4,1,3,2,0:T(8,128)S(1)}, f32[16,8,12,11,128]{4,1,3,2,0:T(8,128)S(1)}) fusion(f32[16,8,12,11,128]{4,1,3,2,0:T(8,128)S(1)} %constant_dynamic-update-slice_fusion.1, f32[16,8,12,8,128]{4,3,2,1,0:T(8,128)} %param.8), kind=kLoop, calls=%fused_computation.46 | loop fusion | bytes 18874368 | tf_op jit(solution)/shard_map/concatenate | solution.py:17
  127.4 2.0 constant_dynamic-update-slice_fusion.2
  129.5 32.5 %multiply_select_fusion = f32[16,8,12,9,128]{4,1,3,2,0:T(8,128)} fusion(f32[16,8,12,11,128]{4,1,3,2,0:T(8,128)S(1)} %constant_dynamic-update-slice_fusion.2, f32[16,8,12,11,128]{4,1,3,2,0:T(8,128)S(1)} %get-tuple-element.48, f32[8,12,128]{2,0,1:T(8,128)S(1)} %copy-done.2, pred[8,12,128]{2,0,1:T(8,128)(4,1)S(1)} %broadcast_compare_fusion), kind=kLoop, calls=%fused_computation.8 | loop fusion | flops 224722944 | bytes 49606656 | tf_op jit(solution)/shard_map/jit(_where)/select_n | solution.py:86
  161.9 8.9 %fusion.27 = f32[16,8,12,8,128]{4,1,3,2,0:T(8,128)S(1)} fusion(f32[16,8,12,9,128]{4,1,3,2,0:T(8,128)} %multiply_select_fusion, f32[16,8,12,8,128]{4,3,2,1,0:T(8,128)S(1)} %bitcast.62), kind=kLoop, calls=%fused_computation.38 | loop fusion | flops 4718592 | bytes 25165824 | tf_op jit(solution)/shard_map/sub | solution.py:87
  171.8 2.4 multiply_subtract_fusion.2
  174.2 2.7 copy-done
  178.1 1.9 gather_fusion
  180.0 2.9 fusion.32
  184.2 70.7 %all-gather.2.cloned.1.call-done = bf16[64,4,12,8,128]{4,3,2,0,1:T(8,128)(2,1)} async-done(((bf16[16,4,12,8,128]{4,3,2,0,1:T(8,128)(2,1)}), bf16[64,4,12,8,128]{4,3,2,0,1:T(8,128)(2,1)}) %all-gather.2.cloned.1.call-update) | async-done | bytes 6291472 | tf_op jit(solution)/shard_map/all_gather | solution.py:94
  254.9 7.1 %copy.34 = bf16[64,4,12,8,128]{4,3,0,2,1:T(8,128)(2,1)} copy(bf16[64,4,12,8,128]{4,3,2,0,1:T(8,128)(2,1)} %all-gather.2.cloned.1.call-done) | data formatting | bytes 12582912 | tf_op jit(solution)/shard_map/while | solution.py:78
  262.0 10.3 %reshape.70 = bf16[64,48,1024]{2,0,1:T(8,128)(2,1)} reshape(bf16[64,4,12,8,128]{4,3,0,2,1:T(8,128)(2,1)} %copy.34) | data formatting | bytes 12582912 | tf_op jit(solution)/shard_map/while | solution.py:78
  272.3 268.3 %while.10 = (s32[]{:T(128)}, bf16[48,16,1024]{2,1,0:T(8,128)(2,1)S(1)}, s32[48]{0:T(128)S(1)}, bf16[64,48,1024]{2,0,1:T(8,128)(2,1)}, bf16[64,1024]{1,0:T(8,128)(2,1)S(1)}, /*index=5*/s32[]{:T(128)}, s32[]{:T(128)}, s32[]{:T(128)}) while((s32[]{:T(128)}, bf16[48,16,1024]{2,1,0:T(8,128)(2,1)S(1)}, s32[48]{0:T(128)S(1)}, ...), condition=%wide.region_1.2_spmd, body=%wide.region_0.1_spmd.sunk | while | flops 138461184 | bytes 5210255 | solution.py:78
  291.3 1.7 convolution_convert_fusion.2
  308.1 1.7 convolution_convert_fusion.2
  330.4 1.7 convolution_convert_fusion.2
  336.0 1.7 convolution_convert_fusion.2
  358.4 1.7 convolution_convert_fusion.2
  375.1 1.7 convolution_convert_fusion.2
  541.1 4.4 bitcast_add_fusion
  545.5 3.8 copy.26
  (268 shorter events, 181.5 us)
Async XLA Ops:
  6.5 248.3 %all-gather.2.cloned.1.call-start = ((), (), s32[]{:S(2)}) async-start(), calls=%async_computation | async-start | bytes 7864320 | tf_op jit(solution)/shard_map/all_gather | solution.py:94
  12.8 9.9 %copy-start.4 = (s32[1,8]{1,0:T(1,128)S(1)}, s32[1,8]{1,0:T(1,128)}, u32[]{:S(2)}) copy-start(s32[1,8]{1,0:T(1,128)} %param.12) | copy-start | bytes 100
  12.8 9.9 %copy-start.3 = (f32[16]{0:T(128)S(1)}, f32[16]{0:T(128)}, u32[]{:S(2)}) copy-start(f32[16]{0:T(128)} %param.10) | copy-start | bytes 196
  12.8 9.9 %copy-start.2 = (f32[8,12,128]{2,0,1:T(8,128)S(1)}, f32[8,12,128]{2,0,1:T(8,128)}, u32[]{:S(2)}) copy-start(f32[8,12,128]{2,0,1:T(8,128)} %param.9) | copy-start | bytes 147460
  13.6 105.9 %collective-permute-start = (f32[16,8,12,3,128]{4,1,3,2,0:T(8,128)S(1)}, f32[16,8,12,3,128]{4,1,3,2,0:T(8,128)S(1)}, u32[]{:S(2)}, u32[]{:S(2)}) collective-permute-start(f32[16,8,12,3,128]{4,1,3,2,0:T(8,128)S(1)} %copy.47), channel_id=1, source_target_pairs={{0,4},{4,8},{8,12},{12,16},{16,20},{20,24},{24,28},{28,32},{32,36}... | collective-permute-start | bytes 7077896 | tf_op jit(solution)/shard_map/ppermute | solution.py:19
  21.4 106.0 %collective-permute-start.1 = (f32[16,8,12,3,128]{4,1,3,2,0:T(8,128)}, f32[16,8,12,3,128]{4,1,3,2,0:T(8,128)}, u32[]{:S(2)}, u32[]{:S(2)}) collective-permute-start(f32[16,8,12,3,128]{4,1,3,2,0:T(8,128)} %copy.46), channel_id=1, source_target_pairs={{4,0},{8,4},{12,8},{16,12},{20,16},{24,20},{28,24},{32,28},{36,32}... | collective-permute-start | bytes 7077896 | tf_op jit(solution)/shard_map/ppermute | solution.py:21
  127.4 34.5 %slice-start = ((s8[6291456]{0:T(1024)(128)(4,1)}), s8[4194304]{0:T(1024)(128)(4,1)S(1)}, s32[]{:S(2)}) async-start(s8[6291456]{0:T(1024)(128)(4,1)} %bitcast.61), calls=%async_computation.1 | async-start | bytes 8388608
  129.4 32.5 %slice-start.1 = ((s8[6291456]{0:T(1024)(128)(4,1)}), s8[2097152]{0:T(1024)(128)(4,1)S(1)}, s32[]{:S(2)}) async-start(s8[6291456]{0:T(1024)(128)(4,1)} %bitcast.61), calls=%async_computation.2 | async-start | bytes 4194304
  174.2 2.7 copy-start
  176.9 6.1 %copy-start.1 = (bf16[64,64,16]{1,2,0:T(8,128)(2,1)S(1)}, bf16[64,64,16]{1,2,0:T(8,128)(2,1)}, u32[]{:S(2)}) copy-start(bf16[64,64,16]{1,2,0:T(8,128)(2,1)} %param.11) | copy-start | bytes 393220
Sparse Core Ops, SparseCore 0:
  183.1 71.7 all-gather.1
where the time goes:
time: 559 us; the launch traced here: 556 us
  waiting for transfers between devices  167 us (30%)
  other arithmetic  125 us (22%)
  matrix products  84 us (15%)
  loops' own time  82.2 us (15%)
  local copies, waits for them, and re-layouts  76.2 us (14%)
  between operations  14.3 us (3%)
  starting transfers between devices  6.91 us (1%)
    ppermute x1, waiting for transfers between devices, padded_2(): lax.ppermute(tail, axis, [(i, (i + 1) % count) for i in range(ends)])  96.8 us
    another operation x1, loops' own time, collide(): result = lax.map(one_plane, jnp.arange(planes, dtype=jnp.int32))  82.2 us
    dot_general x48, matrix products, one_plane(): lax.dot_general(table, cells, (((0,), (0,)), ((), ())), preferred_element...  79.6 us
    all_gather x1, waiting for transfers between devices, local(): whole = lax.all_gather(picked, 'bin', axis=0, tiled=True)  70.7 us
    while x48, other arithmetic  44.6 us
    dot_general x48, other arithmetic, one_plane(): jnp.einsum('ic,ikc->kc', cells, inner, preferred_element_type=jnp.float32)  33.7 us
    select_n x1, other arithmetic, local(): flux = jnp.where(speed > 0, flux_pos, flux_neg)  32.5 us
    dynamic_slice x48, local copies, waits for them, and re-layouts, collide(): result = lax.map(one_plane, jnp.arange(planes, dtype=jnp.int32))  27.8 us
  transfers between devices with their start and end apart: 3, of which 2 were waited for; matrix products, arithmetic and copies ran while one was open for 2% of the time, Pallas kernels for 0%

commit v1 on v0

--- a/solution.py
+++ b/solution.py
@@ -91,7 +91,9 @@
     order = act_order[0, :capacity]
     picked = jnp.take(settled, order, axis=1).astype(jnp.bfloat16)
     all_bins = collection.shape[0]
-    whole = lax.all_gather(picked, "bin", axis=0, tiled=True)
+    whole = jnp.concatenate(
+        lax.all_to_all(jnp.stack([picked] * lax.axis_size("bin")), "bin", 0, 0), axis=0
+    )
     tendency = collide(whole, collection.reshape(all_bins, -1))
     entries = jnp.arange(capacity, dtype=jnp.int32)
     slot_ids = jnp.arange(slots, dtype=jnp.int32)

time: 559 us -> 579 us (1.036)
  loops' own time: 82.2 us -> 101 us
  between operations: 14.3 us -> 0.91 us
  local copies, waits for them, and re-layouts: 76.2 us -> 85.9 us
  starting transfers between devices: 6.91 us -> 13.8 us
    all_gather x1 -> x0, waiting for transfers between devices: 70.7 us -> none  [local(): whole = lax.all_gather(picked, 'bin', axis=0, tiled=True)]
    all_to_all x0 -> x1, waiting for transfers between devices: none -> 68.7 us  [local(): lax.all_to_all(jnp.stack([picked] * lax.axis_size('bin')), 'bin', 0, 0)]
    another operation x1, loops' own time: 82.2 us -> 101 us  [collide(): result = lax.map(one_plane, jnp.arange(planes, dtype=jnp.int32))]
    all_to_all x0 -> x1, starting transfers between devices: none -> 6.88 us  [local(): lax.all_to_all(jnp.stack([picked] * lax.axis_size('bin')), 'bin', 0, 0)]
where the time goes in v1:
time: 579 us; the launch traced here: 575 us
  waiting for transfers between devices  165 us (28%)
  other arithmetic  124 us (21%)
  loops' own time  101 us (17%)
  local copies, waits for them, and re-layouts  85.9 us (15%)
  matrix products  84 us (15%)
  starting transfers between devices  13.8 us (2%)
    another operation x1, loops' own time, collide(): result = lax.map(one_plane, jnp.arange(planes, dtype=jnp.int32))  101 us
    ppermute x1, waiting for transfers between devices, padded_2(): lax.ppermute(tail, axis, [(i, (i + 1) % count) for i in range(ends)])  96.8 us
    dot_general x48, matrix products, one_plane(): lax.dot_general(table, cells, (((0,), (0,)), ((), ())), preferred_element...  79.6 us
    all_to_all x1, waiting for transfers between devices, local(): lax.all_to_all(jnp.stack([picked] * lax.axis_size('bin')), 'bin', 0, 0)  68.7 us
    while x48, other arithmetic  44.6 us
    dot_general x48, other arithmetic, one_plane(): jnp.einsum('ic,ikc->kc', cells, inner, preferred_element_type=jnp.float32)  33.7 us
    select_n x1, other arithmetic, local(): flux = jnp.where(speed > 0, flux_pos, flux_neg)  32.5 us
    dynamic_slice x48, local copies, waits for them, and re-layouts, collide(): result = lax.map(one_plane, jnp.arange(planes, dtype=jnp.int32))  31.9 us
  transfers between devices with their start and end apart: 3, of which 2 were waited for; matrix products, arithmetic and copies ran while one was open for 2% of the time, Pallas kernels for 0%

profile of v1, /device:TPU:1, one launch (start us, length us, event | category | flops | bytes accessed | tf_op | source)
XLA Modules:
  0.0 575.0 jit_solution(1451489985640293401)
XLA Ops:
  0.0 6.3 %fusion.39 = (f32[16,8,12,3,128]{4,3,2,1,0:T(4,128)S(1)}, f32[16,8,12,3,128]{4,3,2,1,0:T(4,128)S(1)}) fusion(f32[16,8,12,8,128]{4,3,2,1,0:T(8,128)} %param.8), kind=kLoop, calls=%fused_computation.63 | loop fusion | bytes 9437184 | tf_op jit(solution)/shard_map/slice | solution.py:16
  7.1 5.6 collective-permute-start
  12.7 2.2 copy.70
  16.2 96.8 %collective-permute-done = f32[16,8,12,3,128]{4,1,3,2,0:T(8,128)S(1)} collective-permute-done((f32[16,8,12,3,128]{4,1,3,2,0:T(8,128)S(1)}, f32[16,8,12,3,128]{4,1,3,2,0:T(8,128)S(1)}, u32[]{:S(2)}, u32[]{:S(2)}) %collective-permute-start) | collective-permute-done | bytes 2359328 | tf_op jit(solution)/shard_map/ppermute | solution.py:19
  113.2 7.7 %constant_dynamic-update-slice_fusion = (f32[16,8,12,11,128]{4,1,3,2,0:T(8,128)S(1)}, f32[16,8,12,11,128]{4,1,3,2,0:T(8,128)S(1)}) fusion(f32[16,8,12,11,128]{4,1,3,2,0:T(8,128)S(1)} %constant_dynamic-update-slice_fusion.1, f32[16,8,12,8,128]{4,3,2,1,0:T(8,128)} %param.8), kind=kLoop, calls=%fused_computation.46 | loop fusion | bytes 18874368 | tf_op jit(solution)/shard_map/concatenate | solution.py:17
  120.9 2.0 constant_dynamic-update-slice_fusion.2
  122.9 32.5 %multiply_select_fusion = f32[16,8,12,9,128]{4,1,3,2,0:T(8,128)} fusion(f32[16,8,12,11,128]{4,1,3,2,0:T(8,128)S(1)} %constant_dynamic-update-slice_fusion.2, f32[16,8,12,11,128]{4,1,3,2,0:T(8,128)S(1)} %get-tuple-element.58, f32[8,12,128]{2,0,1:T(8,128)S(1)} %copy-done.2, pred[8,12,128]{2,0,1:T(8,128)(4,1)S(1)} %broadcast_compare_fusion), kind=kLoop, calls=%fused_computation.8 | loop fusion | flops 224722944 | bytes 49606656 | tf_op jit(solution)/shard_map/jit(_where)/select_n | solution.py:86
  155.4 8.9 %fusion.27 = f32[16,8,12,8,128]{4,1,3,2,0:T(8,128)S(1)} fusion(f32[16,8,12,9,128]{4,1,3,2,0:T(8,128)} %multiply_select_fusion, f32[16,8,12,8,128]{4,3,2,1,0:T(8,128)S(1)} %bitcast.62), kind=kLoop, calls=%fused_computation.38 | loop fusion | flops 4718592 | bytes 25165824 | tf_op jit(solution)/shard_map/sub | solution.py:87
  165.2 2.4 multiply_subtract_fusion.2
  167.6 2.7 copy-done
  171.5 1.9 gather_fusion
  173.5 1.8 fusion.32
  175.7 4.2 stack.2
  179.9 6.9 %all-to-all-start = ((bf16[4,16,4,12,8,128]{5,4,1,3,2,0:T(8,128)(2,1)}), bf16[4,16,4,12,8,128]{5,4,1,3,2,0:T(8,128)(2,1)}, u32[]{:S(2)}, u32[]{:S(2)}) async-start(bf16[4,16,4,12,8,128]{5,4,1,3,2,0:T(8,128)(2,1)} %stack.2), calls=%async_computation | async-start | bytes 12582912 | tf_op jit(solution)/shard_map/all_to_all | solution.py:95
  188.0 68.7 %all-to-all-done = bf16[4,16,4,12,8,128]{5,4,1,3,2,0:T(8,128)(2,1)} async-done(((bf16[4,16,4,12,8,128]{5,4,1,3,2,0:T(8,128)(2,1)}), bf16[4,16,4,12,8,128]{5,4,1,3,2,0:T(8,128)(2,1)}, u32[]{:S(2)}, u32[]{:S(2)}) %all-to-all-start) | async-done | bytes 6291488 | tf_op jit(solution)/shard_map/all_to_all | solution.py:95
  256.7 8.1 %copy.58 = bf16[4,16,4,12,8,128]{5,4,1,0,3,2:T(8,128)(2,1)} copy(bf16[4,16,4,12,8,128]{5,4,1,3,2,0:T(8,128)(2,1)} %all-to-all-done) | data formatting | bytes 12582912 | tf_op jit(solution)/shard_map/while | solution.py:78
  264.7 10.3 %reshape.68 = bf16[64,48,1024]{2,0,1:T(8,128)(2,1)} reshape(bf16[4,16,4,12,8,128]{5,4,1,0,3,2:T(8,128)(2,1)} %copy.58) | data formatting | bytes 12582912 | tf_op jit(solution)/shard_map/while | solution.py:78
  275.0 291.3 %while.10 = (s32[]{:T(128)}, bf16[48,16,1024]{2,1,0:T(8,128)(2,1)S(1)}, s32[48]{0:T(128)S(1)}, bf16[64,48,1024]{2,0,1:T(8,128)(2,1)}, bf16[64,1024]{1,0:T(8,128)(2,1)S(1)}, /*index=5*/s32[]{:T(128)}, s32[]{:T(128)}, s32[]{:T(128)}) while((s32[]{:T(128)}, bf16[48,16,1024]{2,1,0:T(8,128)(2,1)S(1)}, s32[48]{0:T(128)S(1)}, ...), condition=%wide.region_1.2_spmd, body=%wide.region_0.1_spmd.sunk | while | flops 138461184 | bytes 5210255 | solution.py:78
  277.8 1.7 convolution_convert_fusion.2
  283.9 1.7 convolution_convert_fusion.2
  296.0 1.7 convolution_convert_fusion.2
  320.3 1.7 convolution_convert_fusion.2
  566.8 4.4 bitcast_add_fusion
  571.2 3.8 copy.50
  (269 shorter events, 189.4 us)
Async XLA Ops:
  6.3 9.9 %copy-start.4 = (s32[1,8]{1,0:T(1,128)S(1)}, s32[1,8]{1,0:T(1,128)}, u32[]{:S(2)}) copy-start(s32[1,8]{1,0:T(1,128)} %param.12) | copy-start | bytes 100
  6.3 9.9 %copy-start.3 = (f32[16]{0:T(128)S(1)}, f32[16]{0:T(128)}, u32[]{:S(2)}) copy-start(f32[16]{0:T(128)} %param.10) | copy-start | bytes 196
  6.3 9.9 %copy-start.2 = (f32[8,12,128]{2,0,1:T(8,128)S(1)}, f32[8,12,128]{2,0,1:T(8,128)}, u32[]{:S(2)}) copy-start(f32[8,12,128]{2,0,1:T(8,128)} %param.9) | copy-start | bytes 147460
  7.1 105.9 %collective-permute-start = (f32[16,8,12,3,128]{4,1,3,2,0:T(8,128)S(1)}, f32[16,8,12,3,128]{4,1,3,2,0:T(8,128)S(1)}, u32[]{:S(2)}, u32[]{:S(2)}) collective-permute-start(f32[16,8,12,3,128]{4,1,3,2,0:T(8,128)S(1)} %copy.71), channel_id=1, source_target_pairs={{0,4},{4,8},{8,12},{12,16},{16,20},{20,24},{24,28},{28,32},{32,36}... | collective-permute-start | bytes 7077896 | tf_op jit(solution)/shard_map/ppermute | solution.py:19
  14.9 106.0 %collective-permute-start.1 = (f32[16,8,12,3,128]{4,1,3,2,0:T(8,128)}, f32[16,8,12,3,128]{4,1,3,2,0:T(8,128)}, u32[]{:S(2)}, u32[]{:S(2)}) collective-permute-start(f32[16,8,12,3,128]{4,1,3,2,0:T(8,128)} %copy.70), channel_id=1, source_target_pairs={{4,0},{8,4},{12,8},{16,12},{20,16},{24,20},{28,24},{32,28},{36,32}... | collective-permute-start | bytes 7077896 | tf_op jit(solution)/shard_map/ppermute | solution.py:21
  120.9 34.5 %slice-start = ((s8[6291456]{0:T(1024)(128)(4,1)}), s8[4194304]{0:T(1024)(128)(4,1)S(1)}, s32[]{:S(2)}) async-start(s8[6291456]{0:T(1024)(128)(4,1)} %bitcast.61), calls=%async_computation.1 | async-start | bytes 8388608
  122.9 32.5 %slice-start.1 = ((s8[6291456]{0:T(1024)(128)(4,1)}), s8[2097152]{0:T(1024)(128)(4,1)S(1)}, s32[]{:S(2)}) async-start(s8[6291456]{0:T(1024)(128)(4,1)} %bitcast.61), calls=%async_computation.2 | async-start | bytes 4194304
  167.6 2.7 copy-start
  179.9 6.9 %copy-start.1 = (bf16[64,64,16]{1,2,0:T(8,128)(2,1)S(1)}, bf16[64,64,16]{1,2,0:T(8,128)(2,1)}, u32[]{:S(2)}) copy-start(bf16[64,64,16]{1,2,0:T(8,128)(2,1)} %param.11) | copy-start | bytes 393220
  179.9 76.8 %all-to-all-start = ((bf16[4,16,4,12,8,128]{5,4,1,3,2,0:T(8,128)(2,1)}), bf16[4,16,4,12,8,128]{5,4,1,3,2,0:T(8,128)(2,1)}, u32[]{:S(2)}, u32[]{:S(2)}) async-start(bf16[4,16,4,12,8,128]{5,4,1,3,2,0:T(8,128)(2,1)} %stack.2), calls=%async_computation | async-start | bytes 12582912 | tf_op jit(solution)/shard_map/all_to_all | solution.py:95
